TPU v7x, 32 devices: a whole 2x2x4 slice. The times are simulated.
32 devices in a mesh: groups: 2 (over x), lbond: 16 (over z, y, core).
Axes of the slice: x: 2, y: 2, z: 4, core: 2. Of those that a mesh axis runs over, the one named last changes fastest.
Arguments:
- env_in: bfloat16 [4096, 1024], P('lbond', 'groups'), parts along dimension 1, may hold values from -6 to 6
- site_tensors: bfloat16 [4, 4096, 4, 4096], P(None, 'lbond'), may hold values from -0.125 to 0.125
- weight_table: float32 [64, 4], replicated, may hold values from -3 to 3
- state_codes: int32 [4, 1024], P(None, 'groups'), parts along dimension 1, may hold values from 0 to 63
- rescale: int32 [4], replicated, may hold values from 1 to 3
Outputs:
- env_out: bfloat16 [4096, 1024], P('lbond', 'groups'), parts along dimension 1
There are 2 independent parts, one for each index of `groups`. A program takes and returns all parts, laid end to end along the dimension named above; an argument that names none is the same for every part. Nothing has to cross between parts.
All inputs are finite; a program needn't handle non-finite values.
Results may differ from a plain program's by a relative error of at most 0.018.
Values may be sent and summed in bfloat16 or wider, within the bound.
A program may use at most 128 MiB of HBM per device.

v0:
```python
import jax
import jax.numpy as jnp
from jax import lax
from jax.sharding import PartitionSpec as P


def on_device(env_in, site_tensors, weight_table, state_codes, rescale):
    sites = site_tensors.shape[0]
    photon = site_tensors.shape[2]
    entries = weight_table.shape[0]
    matches = (
        state_codes[:, :, None] == jnp.arange(entries, dtype=jnp.int32)[None, None, :]
    ).astype(jnp.float32)
    weights = jnp.einsum("srt,tp->spr", matches, weight_table, precision=lax.Precision.HIGHEST)
    factors = rescale.astype(jnp.float32) * 0.5
    env = env_in
    for index in range(sites):
        mix = weights[index]
        local = env.shape[0]
        width = env.shape[1]
        scaled = (env.astype(jnp.float32)[:, None, :] * mix[None, :, :]).astype(jnp.bfloat16)
        scaled = scaled.reshape(local * photon, width)
        flat = site_tensors[index].reshape(local * photon, -1)
        sums = lax.psum_scatter(
            lax.dot_general(
                flat, scaled, (((0,), (0,)), ((), ())), preferred_element_type=jnp.float32
            ),
            "lbond",
            scatter_dimension=0,
            tiled=True,
        )
        env = (sums * factors[index]).astype(jnp.bfloat16)
    return env


def solution(mesh):
    placed = (P("lbond", "groups"), P(None, "lbond", None, None), P(), P(None, "groups"), P())
    return jax.shard_map(
        on_device, mesh=mesh, in_specs=placed, out_specs=P("lbond", "groups"), check_vma=False
    )
```

profile of v0, /device:TPU:0, one launch (start us, length us, event | category | flops | bytes accessed | tf_op | source)
XLA Modules:
  0.0 528.1 jit_solution(5805313597439892961)
XLA Ops:
  6.5 0.7 copy-done
  7.2 1.0 convolution_bitcast_fusion.4
  8.2 1.0 convert_element_type.80
  9.2 0.4 multiply_convert_fusion.3
  9.9 31.5 %fusion.5 = (bf16[1,256,4,4096]{3,2,1,0:T(4,128)(2,1)}, bf16[1,256,4,4096]{3,2,1,0:T(4,128)(2,1)}, bf16[1,256,4,4096]{3,2,1,0:T(4,128)(2,1)}, bf16[1,256,4,4096]{3,2,1,0:T(4,128)(2,1)}) fusion(bf16[4,256,4,4096]{3,2,1,0:T(4,128)(2,1)} %param.6), kind=kLoop, calls=%fused_computation.24 | loop fusion | bytes 67108864 | tf_op jit(solution)/shard_map/slice | solution.py:23
  41.4 12.5 %reshape_squeeze.12 = bf16[1024,4096]{1,0:T(8,128)(2,1)} reshape(bf16[1,256,4,4096]{3,2,1,0:T(4,128)(2,1)} %get-tuple-element.7) | data formatting | bytes 16777216 | tf_op jit(solution)/shard_map/reshape;squeeze | solution.py:23
  53.9 10.1 %convolution_bitcast_fusion.3 = f32[4096,512]{0,1:T(8,128)} fusion(bf16[1024,512]{1,0:T(8,128)(2,1)S(1)} %convert_element_type.82, bf16[1024,4096]{1,0:T(8,128)(2,1)} %reshape_squeeze.12), kind=kOutput, calls=%fused_computation.3 | convolution fusion | flops 4294967296 | bytes 17825792 | tf_op jit(solution)/shard_map/dot_general | solution.py:25
  64.1 12.7 %reshape_squeeze.13 = bf16[1024,4096]{1,0:T(8,128)(2,1)} reshape(bf16[1,256,4,4096]{3,2,1,0:T(4,128)(2,1)} %get-tuple-element.6) | data formatting | bytes 16777216 | tf_op jit(solution)/shard_map/reshape;squeeze | solution.py:23
  76.8 0.7 fusion.6
  77.5 93.0 %reduce-scatter.5.cloned.1.call-done = f32[256,512]{0,1:T(8,128)} async-done(((f32[4096,512]{0,1:T(8,128)}), f32[256,512]{0,1:T(8,128)}) %reduce-scatter.5.cloned.1.call-update) | async-done | bytes 524304 | tf_op jit(solution)/shard_map/reduce_scatter | solution.py:24
  170.5 1.6 fusion
  173.0 10.2 %convolution_bitcast_fusion.2 = f32[4096,512]{0,1:T(8,128)} fusion(bf16[1024,512]{1,0:T(8,128)(2,1)S(1)} %convert_element_type.87, bf16[1024,4096]{1,0:T(8,128)(2,1)} %reshape_squeeze.13), kind=kOutput, calls=%fused_computation.2 | convolution fusion | flops 4294967296 | bytes 17825792 | tf_op jit(solution)/shard_map/dot_general | solution.py:25
  183.3 13.0 %reshape_squeeze.14 = bf16[1024,4096]{1,0:T(8,128)(2,1)} reshape(bf16[1,256,4,4096]{3,2,1,0:T(4,128)(2,1)} %get-tuple-element.8) | data formatting | bytes 16777216 | tf_op jit(solution)/shard_map/reshape;squeeze | solution.py:23
  196.2 90.4 %reduce-scatter.7.cloned.1.call-done = f32[256,512]{0,1:T(8,128)} async-done(((f32[4096,512]{0,1:T(8,128)}), f32[256,512]{0,1:T(8,128)}) %reduce-scatter.7.cloned.1.call-update) | async-done | bytes 524304 | tf_op jit(solution)/shard_map/reduce_scatter | solution.py:24
  286.6 1.7 fusion.1
  288.5 0.4 multiply_convert_fusion.1
  289.2 10.1 %convolution_bitcast_fusion.1 = f32[4096,512]{0,1:T(8,128)} fusion(bf16[1024,512]{1,0:T(8,128)(2,1)S(1)} %convert_element_type.91, bf16[1024,4096]{1,0:T(8,128)(2,1)} %reshape_squeeze.14), kind=kOutput, calls=%fused_computation.1 | convolution fusion | flops 4294967296 | bytes 17825792 | tf_op jit(solution)/shard_map/dot_general | solution.py:25
  299.6 13.0 %reshape_squeeze.15 = bf16[1024,4096]{1,0:T(8,128)(2,1)} reshape(bf16[1,256,4,4096]{3,2,1,0:T(4,128)(2,1)} %get-tuple-element.5) | data formatting | bytes 16777216 | tf_op jit(solution)/shard_map/reshape;squeeze | solution.py:23
  312.5 90.2 %reduce-scatter.9.cloned.1.call-done = f32[256,512]{0,1:T(8,128)} async-done(((f32[4096,512]{0,1:T(8,128)}), f32[256,512]{0,1:T(8,128)}) %reduce-scatter.9.cloned.1.call-update) | async-done | bytes 524304 | tf_op jit(solution)/shard_map/reduce_scatter | solution.py:24
  402.8 1.8 fusion.2
  405.4 10.2 %convolution_bitcast_fusion = f32[4096,512]{0,1:T(8,128)} fusion(bf16[1024,512]{1,0:T(8,128)(2,1)S(1)} %convert_element_type.95, bf16[1024,4096]{1,0:T(8,128)(2,1)} %reshape_squeeze.15), kind=kOutput, calls=%fused_computation | convolution fusion | flops 4294967296 | bytes 17825792 | tf_op jit(solution)/shard_map/dot_general | solution.py:25
  415.6 103.4 %reduce-scatter.11.cloned.1.call-done = f32[256,512]{0,1:T(8,128)} async-done(((f32[4096,512]{0,1:T(8,128)}), f32[256,512]{0,1:T(8,128)}) %reduce-scatter.11.cloned.1.call-update) | async-done | bytes 524304 | tf_op jit(solution)/shard_map/reduce_scatter | solution.py:24
  519.0 1.7 multiply_convert_fusion.4
  520.7 0.8 copy.9
  (24 shorter events, 2.9 us)
Async XLA Ops:
  6.5 0.7 copy-start
  6.5 164.0 %reduce-scatter.5.cloned.1.call-start = ((), (), s32[]{:S(2)}) async-start(), calls=%async_computation.4 | async-start | bytes 8912896 | tf_op jit(solution)/shard_map/reduce_scatter | solution.py:24
  64.0 222.6 %reduce-scatter.7.cloned.1.call-start = ((), (), s32[]{:S(2)}) async-start(), calls=%async_computation.5 | async-start | bytes 8912896 | tf_op jit(solution)/shard_map/reduce_scatter | solution.py:24
  64.1 12.8 %copy-start.2 = (s32[4]{0:T(128)S(1)}, s32[4]{0:T(128)}, u32[]{:S(2)}) copy-start(s32[4]{0:T(128)} %param.9) | copy-start | bytes 52
  183.2 219.6 %reduce-scatter.9.cloned.1.call-start = ((), (), s32[]{:S(2)}) async-start(), calls=%async_computation.6 | async-start | bytes 8912896 | tf_op jit(solution)/shard_map/reduce_scatter | solution.py:24
  299.3 219.7 %reduce-scatter.11.cloned.1.call-start = ((), (), s32[]{:S(2)}) async-start(), calls=%async_computation.7 | async-start | bytes 8912896 | tf_op jit(solution)/shard_map/reduce_scatter | solution.py:24
  405.4 116.2 %copy-start.1 = (f32[64,4]{0,1:T(4,128)S(1)}, f32[64,4]{0,1:T(4,128)}, u32[]{:S(2)}) copy-start(f32[64,4]{0,1:T(4,128)} %param.7) | copy-start | bytes 3076
Sparse Core Ops, SparseCore 0:
  64.1 106.3 reduce-scatter.4
  183.3 103.2 reduce-scatter.6
  299.5 103.2 reduce-scatter.8
  415.7 103.2 reduce-scatter.10
where the time goes:
time: 530 us; the launch traced here: 528 us
  waiting for transfers between devices  377 us (71%)
  local copies, waits for them, and re-layouts  86.6 us (16%)
  matrix products  41.6 us (8%)
  between operations  13.3 us (3%)
  other arithmetic  9.3 us (2%)
    reduce_scatter x4, waiting for transfers between devices, on_device(): lax.psum_scatter(lax.dot_general(flat, scaled, (((0,), (0,)), ((), ())),...  377 us
    another operation x4, local copies, waits for them, and re-layouts, on_device(): flat = site_tensors[index].reshape(local * photon, -1)  51.1 us
    dot_general x4, matrix products, on_device(): lax.dot_general(flat, scaled, (((0,), (0,)), ((), ())), preferred_element...  40.6 us
    slice x1, local copies, waits for them, and re-layouts, on_device(): flat = site_tensors[index].reshape(local * photon, -1)  31.5 us
  transfers between devices with their start and end apart: 4, of which 4 were waited for; matrix products, arithmetic and copies ran while one was open for 7% of the time, Pallas kernels for 0%

commit v1 on v0

v1 whole, which is shorter than its diff:
```python
import functools

import jax
import jax.numpy as jnp
from jax import lax
from jax.experimental import pallas as pl
from jax.experimental.pallas import tpu as pltpu
from jax.sharding import PartitionSpec as P

CHUNKS = 2
LAG = 2
RING = 4
LANES = 128


def kernel(
    wide, tall, rescale_ref, env_ref, weight_ref, tensor_ref, out_ref,
    raw, packed, spread, scaled, send_a, recv_a, keep_a, send_b, recv_b, keep_b,
    send_z, recv_z, keep_z, raw_sem, sa_sem, ra_sem, sb_sem, rb_sem, sz_sem, rz_sem,
):
    sites, local, photon, _ = tensor_ref.shape
    rows = env_ref.shape[0] // CHUNKS
    depth = local * photon
    pieces = sites * CHUNKS * tall
    me = lax.axis_index("lbond")
    core = lax.rem(me, 2)
    chip = lax.div(me, 2)
    y = lax.rem(chip, wide)
    z = lax.div(chip, wide)
    mate = me + 1 - 2 * core
    across = (z * wide + (wide - 1 - y)) * 2 + core

    def at_z(other):
        return (other * wide + y) * 2 + core

    def target(q):
        return lax.rem(z + 1 + q, tall)

    barrier = pltpu.get_barrier_semaphore()
    peers = [mate] + ([across] if wide > 1 else [])
    peers += [at_z(target(q)) for q in range(tall - 1)]
    for peer in peers:
        pl.semaphore_signal(barrier, inc=1, device_id={"lbond": peer}, device_id_type=pl.DeviceIdType.MESH)

    def fetch(n):
        site = lax.div(n, tall)
        goal = target(lax.rem(n, tall))
        width = raw.shape[-1]
        columns = pl.ds(pl.multiple_of(goal * width, LANES), width)
        slot = lax.rem(n, 2)
        return pltpu.make_async_copy(tensor_ref.at[site, :, :, columns], raw.at[slot], raw_sem.at[slot])

    for n in range(2):
        fetch(jnp.int32(n)).start()

    left = lax.broadcasted_iota(jnp.int32, (local, depth), 0)
    flat = lax.broadcasted_iota(jnp.int32, (local, depth), 1)
    spread[...] = jnp.where(
        (flat >= left * photon) & (flat < left * photon + photon), 1.0, 0.0
    ).astype(jnp.bfloat16)

    def scale_rows(env, site, c):
        mix = weight_ref[site, pl.ds(pl.multiple_of(c * rows, rows), rows), :]
        for k in range(0, depth, LANES):
            piece = jnp.dot(env, spread[:, k : k + LANES], preferred_element_type=jnp.float32)
            scaled[c, :, k : k + LANES] = (piece * mix).astype(jnp.bfloat16)

    for c in range(CHUNKS):
        scale_rows(env_ref[c * rows : (c + 1) * rows, :], 0, c)

    def split(t):
        unit = lax.div(t, tall)
        return lax.div(unit, CHUNKS), lax.rem(unit, CHUNKS), lax.rem(t, tall)

    def to_mate(t):
        slot = lax.rem(t, RING)
        return pltpu.make_async_remote_copy(
            send_a.at[slot], recv_a.at[slot], sa_sem.at[slot], ra_sem.at[slot],
            device_id={"lbond": mate}, device_id_type=pl.DeviceIdType.MESH,
        )

    def to_across(t):
        slot = lax.rem(t, RING)
        return pltpu.make_async_remote_copy(
            send_b.at[slot], recv_b.at[slot], sb_sem.at[slot], rb_sem.at[slot],
            device_id={"lbond": across}, device_id_type=pl.DeviceIdType.MESH,
        )

    def to_owner(site, c, q):
        half = lax.rem(site, 2)
        return pltpu.make_async_remote_copy(
            send_z.at[half, c, q], recv_z.at[half, c, q], sz_sem.at[half, c, q], rz_sem.at[half, c, q],
            device_id={"lbond": at_z(target(q))}, device_id_type=pl.DeviceIdType.MESH,
        )

    pl.semaphore_wait(barrier, len(peers))

    def step(t, carry):
        @pl.when(t < pieces)
        def _():
            site, c, q = split(t)
            goal = target(q)

            @pl.when(c == 0)
            def _():
                n = site * tall + q
                slot = lax.rem(n, 2)
                fetch(n).wait()
                width = packed.shape[-1]
                for b in range(2 * wide):
                    for k in range(0, local, 16):
                        block = raw[slot, k : k + 16, :, b * width : (b + 1) * width]
                        packed[goal, b, k * photon : (k + 16) * photon, :] = block.reshape(16 * photon, width)

                @pl.when(n + 2 < sites * tall)
                def _():
                    fetch(n + 2).start()

            slot = lax.rem(t, RING)
            for b in range(wide):
                send_a[slot, b] = jnp.dot(
                    scaled[c], packed[goal, 2 * b + 1 - core], preferred_element_type=jnp.float32
                ).astype(jnp.bfloat16)
            to_mate(t).start()
            for b in range(wide):
                keep_a[lax.rem(t, 2), b] = jnp.dot(
                    scaled[c], packed[goal, 2 * b + core], preferred_element_type=jnp.float32
                )

        @pl.when((t >= 1) & (t < pieces + 1))
        def _():
            u = t - 1
            slot = lax.rem(u, RING)
            half = lax.rem(u, 2)
            to_mate(u).wait()
            if wide > 1:
                far = wide - 1 - y
                send_b[slot] = (keep_a[half, far] + recv_a[slot, far].astype(jnp.float32)).astype(jnp.bfloat16)
                to_across(u).start()
            keep_b[half] = keep_a[half, y] + recv_a[slot, y].astype(jnp.float32)

        @pl.when((t >= 2) & (t < pieces + 2))
        def _():
            u = t - 2
            site, c, q = split(u)
            total = keep_b[lax.rem(u, 2)]
            if wide > 1:
                to_across(u).wait()
                total = total + recv_b[lax.rem(u, RING)].astype(jnp.float32)

            @pl.when(q < tall - 1)
            def _():
                send_z[lax.rem(site, 2), c, q] = total.astype(jnp.bfloat16)
                to_owner(site, c, q).start()

            @pl.when(q == tall - 1)
            def _():
                keep_z[c] = total

        last = t - 2 - LAG

        @pl.when((last >= 0) & (lax.rem(last + 1, tall) == 0))
        def _():
            site, c, _ = split(last)
            total = keep_z[c]
            for q in range(tall - 1):
                to_owner(site, c, q).wait()
                total = total + recv_z[lax.rem(site, 2), c, q].astype(jnp.float32)
            env = (total * (rescale_ref[site].astype(jnp.float32) * 0.5)).astype(jnp.bfloat16)

            @pl.when(site < sites - 1)
            def _():
                scale_rows(env, site + 1, c)

            @pl.when(site == sites - 1)
            def _():
                out_ref[pl.ds(pl.multiple_of(c * rows, rows), rows), :] = env

        return carry

    lax.fori_loop(0, pieces + 2 + LAG, step, 0)


def on_device(wide, tall, env_in, site_tensors, weight_table, state_codes, rescale):
    sites, local, photon, right = site_tensors.shape
    entries = weight_table.shape[0]
    rows = env_in.shape[1] // CHUNKS
    depth = local * photon
    matches = (
        state_codes[:, :, None] == jnp.arange(entries, dtype=jnp.int32)[None, None, :]
    ).astype(jnp.float32)
    table = jnp.tile(weight_table, (1, LANES // photon))
    weights = jnp.einsum("srt,tl->srl", matches, table, precision=lax.Precision.HIGHEST)
    vmem = pl.BlockSpec(memory_space=pltpu.VMEM)
    half, full = jnp.bfloat16, jnp.float32
    dma = pltpu.SemaphoreType.DMA
    out = pl.pallas_call(
        functools.partial(kernel, wide, tall),
        out_shape=jax.ShapeDtypeStruct((env_in.shape[1], local), half),
        in_specs=[pl.BlockSpec(memory_space=pltpu.SMEM), vmem, vmem, pl.BlockSpec(memory_space=pl.ANY)],
        out_specs=vmem,
        scratch_shapes=[
            pltpu.VMEM((2, local, photon, right // tall), half),
            pltpu.VMEM((tall, 2 * wide, depth, local), half),
            pltpu.VMEM((local, depth), half),
            pltpu.VMEM((CHUNKS, rows, depth), half),
            pltpu.VMEM((RING, wide, rows, local), half),
            pltpu.VMEM((RING, wide, rows, local), half),
            pltpu.VMEM((2, wide, rows, local), full),
            pltpu.VMEM((RING, rows, local), half),
            pltpu.VMEM((RING, rows, local), half),
            pltpu.VMEM((2, rows, local), full),
            pltpu.VMEM((2, CHUNKS, tall - 1, rows, local), half),
            pltpu.VMEM((2, CHUNKS, tall - 1, rows, local), half),
            pltpu.VMEM((CHUNKS, rows, local), full),
            dma((2,)),
            dma((RING,)),
            dma((RING,)),
            dma((RING,)),
            dma((RING,)),
            dma((2, CHUNKS, tall - 1)),
            dma((2, CHUNKS, tall - 1)),
        ],
        compiler_params=pltpu.CompilerParams(
            collective_id=0, has_side_effects=True, vmem_limit_bytes=60 * 1024 * 1024
        ),
    )(rescale, env_in.T, weights, site_tensors)
    return out.T


def solution(mesh):
    wide = max(1, 4 // mesh.shape["groups"])
    tall = mesh.shape["lbond"] // (2 * wide)
    placed = (P("lbond", "groups"), P(None, "lbond", None, None), P(), P(None, "groups"), P())
    return jax.shard_map(
        functools.partial(on_device, wide, tall),
        mesh=mesh, in_specs=placed, out_specs=P("lbond", "groups"), check_vma=False,
    )
```

time: 530 us -> 121 us (0.23)
  waiting for transfers between devices: 377 us -> 0 us
  Pallas kernels: 0 us -> 114 us
  local copies, waits for them, and re-layouts: 86.6 us -> 4.28 us
  matrix products: 41.6 us -> 2.36 us
  between operations: 13.3 us -> 0.01 us
  other arithmetic: 9.3 us -> 0 us
    reduce_scatter x4 -> x0, waiting for transfers between devices: 377 us -> none  [on_device(): lax.psum_scatter(lax.dot_general(flat, scaled, (((0,), (0,)), ((), ())),...]
    pallas_call x0 -> x1, Pallas kernels: none -> 114 us  [on_device(): pl.pallas_call(functools.partial(kernel, wide, tall), out_shape=jax.Shape...]
    another operation x4 -> x1, local copies, waits for them, and re-layouts: 51.1 us -> 0.01 us  [on_device(): table = jnp.tile(weight_table, (1, LANES // photon))]
    dot_general x5 -> x1, matrix products: 41.6 us -> 2.36 us  [on_device(): jnp.einsum('srt,tl->srl', matches, table, precision=lax.Precision.HIGHEST)]
    slice x2 -> x0, local copies, waits for them, and re-layouts: 32.2 us -> none  [the longest x1 31.5 us: on_device(): flat = site_tensors[index].reshape(local * photon, -1)]
    convert_element_type x9 -> x0, other arithmetic: 9.3 us -> none  [the longest x4 6.11 us: on_device(): env.astype(jnp.float32)[:, None, :] * mix[None, :, :]]
  transfers between devices with their start and end apart: 4 -> 0, of which waited for: 4 -> 0; matrix products, arithmetic and copies ran while one was open for 7% -> 0% of each run, Pallas kernels for 0% -> 0%
where the time goes in v1:
time: 121 us
  Pallas kernels  114 us (94%)
  local copies, waits for them, and re-layouts  4.28 us (4%)
  matrix products  2.36 us (2%)
    pallas_call x1, Pallas kernels, on_device(): pl.pallas_call(functools.partial(kernel, wide, tall), out_shape=jax.Shape...  114 us
    unnamed x3, local copies, waits for them, and re-layouts  2.47 us

profile of v1, /device:TPU:0, one launch (start us, length us, event | category | flops | bytes accessed | tf_op | source)
XLA Modules:
  0.0 120.8 jit_solution(16020831233308382374)
XLA Ops:
  0.0 0.0 copy-start
  0.0 0.7 copy-done
  0.7 1.8 %copy.9 = bf16[256,512]{0,1:T(8,128)(2,1)} copy(bf16[256,512]{1,0:T(8,128)(2,1)} %param.5) | data formatting | bytes 524288 | tf_op args[0]
  2.5 2.4 %fusion.1.weight_ref = f32[4,512,128]{2,1,0:T(8,128)} fusion(f32[64,128,1]{0,1,2:T(8,128)S(1)} %bitcast.8, s32[4,512]{1,0:T(4,128)} %param.8), kind=kOutput, calls=%fused_computation.2 | convolution fusion | flops 201588736 | bytes 1089536 | tf_op jit(solution)/shard_map/srt,tl->srl/dot_general | solution.py:193
  4.9 114.1 %shard_map.55 = bf16[512,256]{1,0:T(8,128)(2,1)} custom-call(s32[4]{0:T(128)} %rescale_ref.1, bf16[512,256]{1,0:T(8,128)(2,1)} %bitcast.6, f32[4,512,128]{2,1,0:T(8,128)} %fusion.1.weight_ref, bf16[4,256,4,4096]{3,2,1,0:T(4,128)(2,1)} %tensor_ref.1), custom_call_target="tpu_custom_call" | custom-call | tf_op jit(solution)/shard_map/pallas_call | solution.py:197
  119.0 1.8 %copy.11 = bf16[256,512]{1,0:T(8,128)(2,1)} copy(bf16[256,512]{0,1:T(8,128)(2,1)} %bitcast.7) | data formatting | bytes 524288 | tf_op jit(solution)/shard_map/transpose | solution.py:228
  (1 shorter events, 0.0 us)
Async XLA Ops:
  0.0 0.7 copy-start

commit v2 on v1

--- a/solution.py
+++ b/solution.py
@@ -8,8 +8,10 @@
 from jax.sharding import PartitionSpec as P
 
 CHUNKS = 2
-LAG = 2
+LAG = 1
+HOLD = 3
 RING = 4
+RING_B = 2 * HOLD
 LANES = 128
 
 
@@ -80,7 +82,7 @@
         )
 
     def to_across(t):
-        slot = lax.rem(t, RING)
+        slot = lax.rem(t, RING_B)
         return pltpu.make_async_remote_copy(
             send_b.at[slot], recv_b.at[slot], sb_sem.at[slot], rb_sem.at[slot],
             device_id={"lbond": across}, device_id_type=pl.DeviceIdType.MESH,
@@ -135,18 +137,18 @@
             to_mate(u).wait()
             if wide > 1:
                 far = wide - 1 - y
-                send_b[slot] = (keep_a[half, far] + recv_a[slot, far].astype(jnp.float32)).astype(jnp.bfloat16)
+                send_b[lax.rem(u, RING_B)] = (keep_a[half, far] + recv_a[slot, far].astype(jnp.float32)).astype(jnp.bfloat16)
                 to_across(u).start()
-            keep_b[half] = keep_a[half, y] + recv_a[slot, y].astype(jnp.float32)
-
-        @pl.when((t >= 2) & (t < pieces + 2))
-        def _():
-            u = t - 2
+            keep_b[lax.rem(u, HOLD)] = keep_a[half, y] + recv_a[slot, y].astype(jnp.float32)
+
+        @pl.when((t >= HOLD) & (t < pieces + HOLD))
+        def _():
+            u = t - HOLD
             site, c, q = split(u)
-            total = keep_b[lax.rem(u, 2)]
+            total = keep_b[lax.rem(u, HOLD)]
             if wide > 1:
                 to_across(u).wait()
-                total = total + recv_b[lax.rem(u, RING)].astype(jnp.float32)
+                total = total + recv_b[lax.rem(u, RING_B)].astype(jnp.float32)
 
             @pl.when(q < tall - 1)
             def _():
@@ -157,7 +159,7 @@
             def _():
                 keep_z[c] = total
 
-        last = t - 2 - LAG
+        last = t - HOLD - LAG
 
         @pl.when((last >= 0) & (lax.rem(last + 1, tall) == 0))
         def _():
@@ -178,7 +180,7 @@
 
         return carry
 
-    lax.fori_loop(0, pieces + 2 + LAG, step, 0)
+    lax.fori_loop(0, pieces + HOLD + LAG, step, 0)
 
 
 def on_device(wide, tall, env_in, site_tensors, weight_table, state_codes, rescale):
@@ -207,17 +209,17 @@
             pltpu.VMEM((RING, wide, rows, local), half),
             pltpu.VMEM((RING, wide, rows, local), half),
             pltpu.VMEM((2, wide, rows, local), full),
-            pltpu.VMEM((RING, rows, local), half),
-            pltpu.VMEM((RING, rows, local), half),
-            pltpu.VMEM((2, rows, local), full),
+            pltpu.VMEM((RING_B, rows, local), half),
+            pltpu.VMEM((RING_B, rows, local), half),
+            pltpu.VMEM((HOLD, rows, local), full),
             pltpu.VMEM((2, CHUNKS, tall - 1, rows, local), half),
             pltpu.VMEM((2, CHUNKS, tall - 1, rows, local), half),
             pltpu.VMEM((CHUNKS, rows, local), full),
             dma((2,)),
             dma((RING,)),
             dma((RING,)),
-            dma((RING,)),
-            dma((RING,)),
+            dma((RING_B,)),
+            dma((RING_B,)),
             dma((2, CHUNKS, tall - 1)),
             dma((2, CHUNKS, tall - 1)),
         ],

time: 121 us -> 116 us (0.959)
  Pallas kernels: 114 us -> 109 us
    pallas_call x1, Pallas kernels: 114 us -> 109 us  [on_device(): pl.pallas_call(functools.partial(kernel, wide, tall), out_shape=jax.Shape...]
where the time goes in v2:
time: 116 us
  Pallas kernels  109 us (94%)
  local copies, waits for them, and re-layouts  4.28 us (4%)
  matrix products  2.36 us (2%)
    pallas_call x1, Pallas kernels, on_device(): pl.pallas_call(functools.partial(kernel, wide, tall), out_shape=jax.Shape...  109 us
    unnamed x3, local copies, waits for them, and re-layouts  2.47 us
    dot_general x1, matrix products, on_device(): jnp.einsum('srt,tl->srl', matches, table, precision=lax.Precision.HIGHEST)  2.36 us

profile of v2, /device:TPU:0, one launch (start us, length us, event | category | flops | bytes accessed | tf_op | source)
XLA Modules:
  0.0 115.7 jit_solution(2682579898520553489)
XLA Ops:
  0.0 0.0 copy-start
  0.0 0.7 copy-done
  0.7 1.8 %copy.9 = bf16[256,512]{0,1:T(8,128)(2,1)} copy(bf16[256,512]{1,0:T(8,128)(2,1)} %param.5) | data formatting | bytes 524288 | tf_op args[0]
  2.5 2.4 %fusion.1.weight_ref = f32[4,512,128]{2,1,0:T(8,128)} fusion(f32[64,128,1]{0,1,2:T(8,128)S(1)} %bitcast.8, s32[4,512]{1,0:T(4,128)} %param.8), kind=kOutput, calls=%fused_computation.2 | convolution fusion | flops 201588736 | bytes 1089536 | tf_op jit(solution)/shard_map/srt,tl->srl/dot_general | solution.py:195
  4.9 109.0 %shard_map.55 = bf16[512,256]{1,0:T(8,128)(2,1)} custom-call(s32[4]{0:T(128)} %rescale_ref.1, bf16[512,256]{1,0:T(8,128)(2,1)} %bitcast.6, f32[4,512,128]{2,1,0:T(8,128)} %fusion.1.weight_ref, bf16[4,256,4,4096]{3,2,1,0:T(4,128)(2,1)} %tensor_ref.1), custom_call_target="tpu_custom_call" | custom-call | tf_op jit(solution)/shard_map/pallas_call | solution.py:199
  113.9 1.8 %copy.11 = bf16[256,512]{1,0:T(8,128)(2,1)} copy(bf16[256,512]{0,1:T(8,128)(2,1)} %bitcast.7) | data formatting | bytes 524288 | tf_op jit(solution)/shard_map/transpose | solution.py:230
  (1 shorter events, 0.0 us)
Async XLA Ops:
  0.0 0.7 copy-start

commit v3 on v2

--- a/solution.py
+++ b/solution.py
@@ -16,12 +16,12 @@
 
 
 def kernel(
-    wide, tall, rescale_ref, env_ref, weight_ref, tensor_ref, out_ref,
+    wide, tall, rescale_ref, env_ref, code_ref, table_ref, tensor_ref, out_ref,
     raw, packed, spread, scaled, send_a, recv_a, keep_a, send_b, recv_b, keep_b,
     send_z, recv_z, keep_z, raw_sem, sa_sem, ra_sem, sb_sem, rb_sem, sz_sem, rz_sem,
 ):
     sites, local, photon, _ = tensor_ref.shape
-    rows = env_ref.shape[0] // CHUNKS
+    rows = env_ref.shape[1] // CHUNKS
     depth = local * photon
     pieces = sites * CHUNKS * tall
     me = lax.axis_index("lbond")
@@ -61,14 +61,30 @@
         (flat >= left * photon) & (flat < left * photon + photon), 1.0, 0.0
     ).astype(jnp.bfloat16)
 
-    def scale_rows(env, site, c):
-        mix = weight_ref[site, pl.ds(pl.multiple_of(c * rows, rows), rows), :]
+    def scale_rows(env, flip, site, c):
+        codes = code_ref[pl.ds(site, 1), pl.ds(pl.multiple_of(c * rows, rows), rows)]
+        entries = table_ref.shape[0]
+        index = lax.broadcasted_iota(jnp.int32, (entries, rows), 0)
+        match = jnp.where(index == codes, 1.0, 0.0).astype(jnp.bfloat16)
+        mix = jnp.zeros((rows, LANES), jnp.float32)
+        rest = table_ref[...]
+        terms = []
+        for _ in range(3):
+            term = rest.astype(jnp.bfloat16)
+            rest = rest - term.astype(jnp.float32)
+            terms.append(term)
+        for term in reversed(terms):
+            mix = mix + lax.dot_general(
+                match, term, (((0,), (0,)), ((), ())), preferred_element_type=jnp.float32
+            )
         for k in range(0, depth, LANES):
-            piece = jnp.dot(env, spread[:, k : k + LANES], preferred_element_type=jnp.float32)
+            piece = lax.dot_general(
+                env, spread[:, k : k + LANES], (((0 if flip else 1,), (0,)), ((), ())),
+                preferred_element_type=jnp.float32,
+            )
             scaled[c, :, k : k + LANES] = (piece * mix).astype(jnp.bfloat16)
 
-    for c in range(CHUNKS):
-        scale_rows(env_ref[c * rows : (c + 1) * rows, :], 0, c)
+    scale_rows(env_ref[:, :rows], True, 0, 0)
 
     def split(t):
         unit = lax.div(t, tall)
@@ -129,6 +145,11 @@
                     scaled[c], packed[goal, 2 * b + core], preferred_element_type=jnp.float32
                 )
 
+        for c in range(1, CHUNKS):
+            @pl.when(t == c * tall - 1)
+            def _():
+                scale_rows(env_ref[:, c * rows : (c + 1) * rows], True, 0, c)
+
         @pl.when((t >= 1) & (t < pieces + 1))
         def _():
             u = t - 1
@@ -172,7 +193,7 @@
 
             @pl.when(site < sites - 1)
             def _():
-                scale_rows(env, site + 1, c)
+                scale_rows(env, False, site + 1, c)
 
             @pl.when(site == sites - 1)
             def _():
@@ -185,21 +206,16 @@
 
 def on_device(wide, tall, env_in, site_tensors, weight_table, state_codes, rescale):
     sites, local, photon, right = site_tensors.shape
-    entries = weight_table.shape[0]
     rows = env_in.shape[1] // CHUNKS
     depth = local * photon
-    matches = (
-        state_codes[:, :, None] == jnp.arange(entries, dtype=jnp.int32)[None, None, :]
-    ).astype(jnp.float32)
     table = jnp.tile(weight_table, (1, LANES // photon))
-    weights = jnp.einsum("srt,tl->srl", matches, table, precision=lax.Precision.HIGHEST)
     vmem = pl.BlockSpec(memory_space=pltpu.VMEM)
     half, full = jnp.bfloat16, jnp.float32
     dma = pltpu.SemaphoreType.DMA
     out = pl.pallas_call(
         functools.partial(kernel, wide, tall),
         out_shape=jax.ShapeDtypeStruct((env_in.shape[1], local), half),
-        in_specs=[pl.BlockSpec(memory_space=pltpu.SMEM), vmem, vmem, pl.BlockSpec(memory_space=pl.ANY)],
+        in_specs=[pl.BlockSpec(memory_space=pltpu.SMEM), vmem, vmem, vmem, pl.BlockSpec(memory_space=pl.ANY)],
         out_specs=vmem,
         scratch_shapes=[
             pltpu.VMEM((2, local, photon, right // tall), half),
@@ -226,7 +242,7 @@
         compiler_params=pltpu.CompilerParams(
             collective_id=0, has_side_effects=True, vmem_limit_bytes=60 * 1024 * 1024
         ),
-    )(rescale, env_in.T, weights, site_tensors)
+    )(rescale, env_in, state_codes, table, site_tensors)
     return out.T
 
 

time: 116 us -> 110 us (0.948)
  matrix products: 2.36 us -> 0 us
  Pallas kernels: 109 us -> 107 us
    unnamed x3 -> x0, local copies, waits for them, and re-layouts: 2.47 us -> none
    dot_general x1 -> x0, matrix products: 2.36 us -> none  [on_device(): jnp.einsum('srt,tl->srl', matches, table, precision=lax.Precision.HIGHEST)]
    pallas_call x1, Pallas kernels: 109 us -> 107 us  [on_device(): pl.pallas_call(functools.partial(kernel, wide, tall), out_shape=jax.Shape...]
    another operation x1 -> x2, local copies, waits for them, and re-layouts: 0.01 us -> 1.39 us  [on_device(): table = jnp.tile(weight_table, (1, LANES // photon))]
where the time goes in v3:
time: 110 us
  Pallas kernels  107 us (97%)
  local copies, waits for them, and re-layouts  3.18 us (3%)
    pallas_call x1, Pallas kernels, on_device(): pl.pallas_call(functools.partial(kernel, wide, tall), out_shape=jax.Shape...  107 us

profile of v3, /device:TPU:0, one launch (start us, length us, event | category | flops | bytes accessed | tf_op | source)
XLA Modules:
  0.0 109.9 jit_solution(9452822101261909167)
XLA Ops:
  0.0 0.7 tile.4
  0.7 0.7 copy.8.table_ref
  1.4 106.7 %shard_map.55 = bf16[512,256]{1,0:T(8,128)(2,1)} custom-call(s32[4]{0:T(128)} %rescale_ref.1, bf16[256,512]{1,0:T(8,128)(2,1)} %env_ref.1, s32[4,512]{1,0:T(4,128)} %code_ref.1, f32[64,128]{1,0:T(8,128)} %copy.8.table_ref, bf16[4,256,4,4096]{3,2,1,0:T(4,128)(2,1)} %tensor_ref.1), custom_call_target="tpu_custom_call" | custom-call | tf_op jit(solution)/shard_map/pallas_call | solution.py:215
  108.1 1.8 %copy.9 = bf16[256,512]{1,0:T(8,128)(2,1)} copy(bf16[256,512]{0,1:T(8,128)(2,1)} %bitcast.2) | data formatting | bytes 524288 | tf_op jit(solution)/shard_map/transpose | solution.py:246

commit v4 on v3

--- a/solution.py
+++ b/solution.py
@@ -7,11 +7,12 @@
 from jax.experimental.pallas import tpu as pltpu
 from jax.sharding import PartitionSpec as P
 
-CHUNKS = 2
-LAG = 1
-HOLD = 3
-RING = 4
-RING_B = 2 * HOLD
+CHUNKS = 4
+HELD_A = 1
+HELD_B = 4
+LAG = 4
+RING_A = 2 * HELD_A + 2
+RING_B = 2 * (HELD_B - HELD_A) + 2
 LANES = 128
 
 
@@ -62,7 +63,10 @@
     ).astype(jnp.bfloat16)
 
     def scale_rows(env, flip, site, c):
-        codes = code_ref[pl.ds(site, 1), pl.ds(pl.multiple_of(c * rows, rows), rows)]
+        line = code_ref[pl.ds(site, 1), :]
+        codes = line[:, :rows]
+        for k in range(1, CHUNKS):
+            codes = jnp.where(c == k, line[:, k * rows : (k + 1) * rows], codes)
         entries = table_ref.shape[0]
         index = lax.broadcasted_iota(jnp.int32, (entries, rows), 0)
         match = jnp.where(index == codes, 1.0, 0.0).astype(jnp.bfloat16)
@@ -91,7 +95,7 @@
         return lax.div(unit, CHUNKS), lax.rem(unit, CHUNKS), lax.rem(t, tall)
 
     def to_mate(t):
-        slot = lax.rem(t, RING)
+        slot = lax.rem(t, RING_A)
         return pltpu.make_async_remote_copy(
             send_a.at[slot], recv_a.at[slot], sa_sem.at[slot], ra_sem.at[slot],
             device_id={"lbond": mate}, device_id_type=pl.DeviceIdType.MESH,
@@ -134,14 +138,14 @@
                 def _():
                     fetch(n + 2).start()
 
-            slot = lax.rem(t, RING)
+            slot = lax.rem(t, RING_A)
             for b in range(wide):
                 send_a[slot, b] = jnp.dot(
                     scaled[c], packed[goal, 2 * b + 1 - core], preferred_element_type=jnp.float32
                 ).astype(jnp.bfloat16)
             to_mate(t).start()
             for b in range(wide):
-                keep_a[lax.rem(t, 2), b] = jnp.dot(
+                keep_a[lax.rem(t, HELD_A + 1), b] = jnp.dot(
                     scaled[c], packed[goal, 2 * b + core], preferred_element_type=jnp.float32
                 )
 
@@ -150,23 +154,23 @@
             def _():
                 scale_rows(env_ref[:, c * rows : (c + 1) * rows], True, 0, c)
 
-        @pl.when((t >= 1) & (t < pieces + 1))
-        def _():
-            u = t - 1
-            slot = lax.rem(u, RING)
-            half = lax.rem(u, 2)
+        @pl.when((t >= HELD_A) & (t < pieces + HELD_A))
+        def _():
+            u = t - HELD_A
+            slot = lax.rem(u, RING_A)
+            half = lax.rem(u, HELD_A + 1)
             to_mate(u).wait()
             if wide > 1:
                 far = wide - 1 - y
                 send_b[lax.rem(u, RING_B)] = (keep_a[half, far] + recv_a[slot, far].astype(jnp.float32)).astype(jnp.bfloat16)
                 to_across(u).start()
-            keep_b[lax.rem(u, HOLD)] = keep_a[half, y] + recv_a[slot, y].astype(jnp.float32)
-
-        @pl.when((t >= HOLD) & (t < pieces + HOLD))
-        def _():
-            u = t - HOLD
+            keep_b[lax.rem(u, HELD_B - HELD_A + 1)] = keep_a[half, y] + recv_a[slot, y].astype(jnp.float32)
+
+        @pl.when((t >= HELD_B) & (t < pieces + HELD_B))
+        def _():
+            u = t - HELD_B
             site, c, q = split(u)
-            total = keep_b[lax.rem(u, HOLD)]
+            total = keep_b[lax.rem(u, HELD_B - HELD_A + 1)]
             if wide > 1:
                 to_across(u).wait()
                 total = total + recv_b[lax.rem(u, RING_B)].astype(jnp.float32)
@@ -180,7 +184,7 @@
             def _():
                 keep_z[c] = total
 
-        last = t - HOLD - LAG
+        last = t - HELD_B - LAG
 
         @pl.when((last >= 0) & (lax.rem(last + 1, tall) == 0))
         def _():
@@ -201,7 +205,7 @@
 
         return carry
 
-    lax.fori_loop(0, pieces + HOLD + LAG, step, 0)
+    lax.fori_loop(0, pieces + HELD_B + LAG, step, 0)
 
 
 def on_device(wide, tall, env_in, site_tensors, weight_table, state_codes, rescale):
@@ -222,18 +226,18 @@
             pltpu.VMEM((tall, 2 * wide, depth, local), half),
             pltpu.VMEM((local, depth), half),
             pltpu.VMEM((CHUNKS, rows, depth), half),
-            pltpu.VMEM((RING, wide, rows, local), half),
-            pltpu.VMEM((RING, wide, rows, local), half),
-            pltpu.VMEM((2, wide, rows, local), full),
+            pltpu.VMEM((RING_A, wide, rows, local), half),
+            pltpu.VMEM((RING_A, wide, rows, local), half),
+            pltpu.VMEM((HELD_A + 1, wide, rows, local), full),
             pltpu.VMEM((RING_B, rows, local), half),
             pltpu.VMEM((RING_B, rows, local), half),
-            pltpu.VMEM((HOLD, rows, local), full),
+            pltpu.VMEM((HELD_B - HELD_A + 1, rows, local), full),
             pltpu.VMEM((2, CHUNKS, tall - 1, rows, local), half),
             pltpu.VMEM((2, CHUNKS, tall - 1, rows, local), half),
             pltpu.VMEM((CHUNKS, rows, local), full),
             dma((2,)),
-            dma((RING,)),
-            dma((RING,)),
+            dma((RING_A,)),
+            dma((RING_A,)),
             dma((RING_B,)),
             dma((RING_B,)),
             dma((2, CHUNKS, tall - 1)),

time: 110 us -> 108 us (0.982)
  Pallas kernels: 107 us -> 105 us
    pallas_call x1, Pallas kernels: 107 us -> 105 us  [on_device(): pl.pallas_call(functools.partial(kernel, wide, tall), out_shape=jax.Shape...]
where the time goes in v4:
time: 108 us
  Pallas kernels  105 us (97%)
  local copies, waits for them, and re-layouts  3.18 us (3%)
    pallas_call x1, Pallas kernels, on_device(): pl.pallas_call(functools.partial(kernel, wide, tall), out_shape=jax.Shape...  105 us

profile of v4, /device:TPU:0, one launch (start us, length us, event | category | flops | bytes accessed | tf_op | source)
XLA Modules:
  0.0 107.8 jit_solution(15264732007881216968)
XLA Ops:
  0.0 0.7 tile.4
  0.7 0.7 copy.8.table_ref
  1.4 104.6 %shard_map.55 = bf16[512,256]{1,0:T(8,128)(2,1)} custom-call(s32[4]{0:T(128)} %rescale_ref.1, bf16[256,512]{1,0:T(8,128)(2,1)} %env_ref.1, s32[4,512]{1,0:T(4,128)} %code_ref.1, f32[64,128]{1,0:T(8,128)} %copy.8.table_ref, bf16[4,256,4,4096]{3,2,1,0:T(4,128)(2,1)} %tensor_ref.1), custom_call_target="tpu_custom_call" | custom-call | tf_op jit(solution)/shard_map/pallas_call | solution.py:219
  106.0 1.8 %copy.9 = bf16[256,512]{1,0:T(8,128)(2,1)} copy(bf16[256,512]{0,1:T(8,128)(2,1)} %bitcast.2) | data formatting | bytes 524288 | tf_op jit(solution)/shard_map/transpose | solution.py:250

commit v5 on v4

--- a/solution.py
+++ b/solution.py
@@ -117,6 +117,17 @@
 
     pl.semaphore_wait(barrier, len(peers))
 
+
+    def repack(n, goal, which):
+        slot = lax.rem(n, 2)
+        width = packed.shape[-1]
+        for b in range(wide):
+            part = 2 * b + which
+            lanes = pl.ds(pl.multiple_of(part * width, LANES), width)
+            for k in range(0, local, 16):
+                block = raw[slot, k : k + 16, :, lanes]
+                packed[goal, part, k * photon : (k + 16) * photon, :] = block.reshape(16 * photon, width)
+
     def step(t, carry):
         @pl.when(t < pieces)
         def _():
@@ -126,17 +137,9 @@
             @pl.when(c == 0)
             def _():
                 n = site * tall + q
-                slot = lax.rem(n, 2)
                 fetch(n).wait()
-                width = packed.shape[-1]
-                for b in range(2 * wide):
-                    for k in range(0, local, 16):
-                        block = raw[slot, k : k + 16, :, b * width : (b + 1) * width]
-                        packed[goal, b, k * photon : (k + 16) * photon, :] = block.reshape(16 * photon, width)
-
-                @pl.when(n + 2 < sites * tall)
-                def _():
-                    fetch(n + 2).start()
+                repack(n, goal, 1 - core)
+
 
             slot = lax.rem(t, RING_A)
             for b in range(wide):
@@ -144,6 +147,16 @@
                     scaled[c], packed[goal, 2 * b + 1 - core], preferred_element_type=jnp.float32
                 ).astype(jnp.bfloat16)
             to_mate(t).start()
+
+            @pl.when(c == 0)
+            def _():
+                n = site * tall + q
+                repack(n, goal, core)
+
+                @pl.when(n + 2 < sites * tall)
+                def _():
+                    fetch(n + 2).start()
+
             for b in range(wide):
                 keep_a[lax.rem(t, HELD_A + 1), b] = jnp.dot(
                     scaled[c], packed[goal, 2 * b + core], preferred_element_type=jnp.float32
@@ -201,7 +214,7 @@
 
             @pl.when(site == sites - 1)
             def _():
-                out_ref[pl.ds(pl.multiple_of(c * rows, rows), rows), :] = env
+                out_ref[:, pl.ds(pl.multiple_of(c * rows, rows), rows)] = jnp.transpose(env)
 
         return carry
 
@@ -218,7 +231,7 @@
     dma = pltpu.SemaphoreType.DMA
     out = pl.pallas_call(
         functools.partial(kernel, wide, tall),
-        out_shape=jax.ShapeDtypeStruct((env_in.shape[1], local), half),
+        out_shape=jax.ShapeDtypeStruct((local, env_in.shape[1]), half),
         in_specs=[pl.BlockSpec(memory_space=pltpu.SMEM), vmem, vmem, vmem, pl.BlockSpec(memory_space=pl.ANY)],
         out_specs=vmem,
         scratch_shapes=[
@@ -247,7 +260,7 @@
             collective_id=0, has_side_effects=True, vmem_limit_bytes=60 * 1024 * 1024
         ),
     )(rescale, env_in, state_codes, table, site_tensors)
-    return out.T
+    return out
 
 
 def solution(mesh):

time: 108 us -> 108 us (level)
    transpose x1 -> x0, local copies, waits for them, and re-layouts: 1.8 us -> none  [on_device(): return out.T]
    unnamed x0 -> x1, local copies, waits for them, and re-layouts: none -> 1.67 us
where the time goes in v5:
time: 108 us
  Pallas kernels  104 us (96%)
  local copies, waits for them, and re-layouts  3.06 us (3%)
    pallas_call x1, Pallas kernels, on_device(): pl.pallas_call(functools.partial(kernel, wide, tall), out_shape=jax.Shape...  104 us

profile of v5, /device:TPU:0, one launch (start us, length us, event | category | flops | bytes accessed | tf_op | source)
XLA Modules:
  0.0 107.5 jit_solution(7741710264327053001)
XLA Ops:
  0.0 0.7 tile.4
  0.7 0.7 copy.7.table_ref
  1.4 104.5 %shard_map.55 = bf16[256,512]{1,0:T(8,128)(2,1)} custom-call(s32[4]{0:T(128)} %rescale_ref.1, bf16[256,512]{1,0:T(8,128)(2,1)} %env_ref.1, s32[4,512]{1,0:T(4,128)} %code_ref.1, f32[64,128]{1,0:T(8,128)} %copy.7.table_ref, bf16[4,256,4,4096]{3,2,1,0:T(4,128)(2,1)} %tensor_ref.1), custom_call_target="tpu_custom_call" | custom-call | tf_op jit(solution)/shard_map/pallas_call | solution.py:232
  105.9 1.7 %copy.9 = bf16[256,512]{1,0:T(8,128)(2,1)} copy(bf16[256,512]{1,0:T(8,128)(2,1)} %shard_map.55) | data formatting | bytes 524288
